TPU v7x, 256 devices: a whole 4x4x8 slice. The times are simulated.
256 devices in a mesh: depth: 32 (over z, x), tile: 8 (over y, core).
Axes of the slice: x: 4, y: 4, z: 8, core: 2. Of those that a mesh axis runs over, the one named last changes fastest.
Arguments:
- tidal: float32 [32, 3, 131072], P('depth', None, 'tile'), may hold values from -1.5 to 1.5
- plane_weight: float32 [32], P('depth'), may hold values from 0.2 to 1
- plane_step: float32 [32], P('depth'), may hold values from 0.2 to 0.6
- ray_angle: float32 [131072], P('tile'), may hold values from -3.140625 to 3.140625
- dest_tile: int32 [32, 1024, 1], P('depth', 'tile'), may hold values from 0 to 7; in each aligned block of 128 rows (0 to 127, 128 to 255, ..., all dimensions but the last counted through in order) at most 32 rows name the same one
- dest_segment: int32 [32, 1024], P('depth', 'tile'), may hold values from 0 to 255
- interp: bfloat16 [32, 1024, 128, 128], P('depth', 'tile'), may hold values from -0.5 to 0.5
Outputs:
- potential_adjoint: float32 [32, 16, 16384], P('depth', 'tile')
Inputs may be any that keep to these rules, and one draw needn't show every extreme that they name: `dest_tile`: in each plane, the 128 blocks of one strip name no strip more than 32 times, a bound that some block reaches.
All inputs are finite; a program needn't handle non-finite values.
Results may differ from a plain program's by a relative error of at most 0.003.
Values sent between devices are 32-bit elements; how exact they have to be, the bound alone decides.
A program may use at most 64 MiB of HBM per device.

v0:
```python
import jax
import jax.numpy as jnp
from jax import lax
from jax.sharding import PartitionSpec as P

ROWS = 2
COLS = 16384


def from_behind(value, axis, steps):
    count = lax.axis_size(axis)
    leading, last = (max(0, -steps), min(count, count - steps))
    return lax.ppermute(value, axis, [(source, source + steps) for source in range(leading, last)])


def padded_2(shard, sides, width):
    for axis, dim in sides:
        count, length = (lax.axis_size(axis), shard.shape[dim])
        up = [(i, (i + 1) % count) for i in range(count - 1)]
        down = [(j, i) for i, j in up]
        last = lax.slice_in_dim(shard, length - width, length, axis=dim)
        leading = lax.slice_in_dim(shard, 0, width, axis=dim)
        before = lax.ppermute(last, axis, up)
        after = lax.ppermute(leading, axis, down)
        shard = jnp.concatenate([before, shard, after], axis=dim)
    return shard


def column_part(field):
    padded = jnp.pad(field, ((0, 0), (0, 0), (1, 1)))
    return 0.5 * (padded[:, :, :-2] - padded[:, :, 2:])


def smooth_cols(field):
    padded = jnp.pad(field, ((0, 0), (0, 0), (1, 1)))
    return 0.25 * padded[:, :, :-2] + 0.5 * field + 0.25 * padded[:, :, 2:]


def per_device(tidal, plane_weight, plane_step, ray_angle, dest_tile, dest_segment, interp):
    planes_here = tidal.shape[0]
    n_tile = lax.axis_size("tile")
    n_depth = lax.axis_size("depth")
    blocks_here = interp.shape[1]
    width = interp.shape[2]
    slots = 2 * blocks_here // n_tile
    segments = ROWS * COLS // width
    jxx = tidal[:, 0]
    jxy = tidal[:, 1]
    jyy = tidal[:, 2]
    local_terms = jnp.stack(
        [
            -jnp.sum(plane_weight[:, None] * (jxx - jyy) * 0.5, axis=0),
            -jnp.sum(plane_weight[:, None] * jxy, axis=0),
        ]
    )
    shear = lax.psum(local_terms, "depth")
    cross = -shear[0] * jnp.sin(2.0 * ray_angle) + shear[1] * jnp.cos(2.0 * ray_angle)
    seed_state = jnp.stack(
        [
            cross * jnp.cos(ray_angle),
            cross * jnp.sin(ray_angle),
            jnp.zeros_like(cross),
            jnp.zeros_like(cross),
        ]
    )

    def sweep(top):
        xb_one, xb_two, tb_one, tb_two = (top[0], top[1], top[2], top[3])
        step_len = plane_step[0]
        tp_one = tb_one + step_len * xb_one
        tp_two = tb_two + step_len * xb_two
        adjoints = [jnp.stack([-tp_one, -tp_two])]
        new_one = xb_one - (jxx[0] * tp_one + jxy[0] * tp_two)
        new_two = xb_two - (jxy[0] * tp_one + jyy[0] * tp_two)
        return (jnp.stack([new_one, new_two, tp_one, tp_two]), jnp.stack(adjoints[::-1]))

    is_last = lax.axis_index("depth") == n_depth - 1

    def relay_step(turn, top):
        bottom, unused = sweep(top)
        incoming = from_behind(bottom, "depth", -1)
        return jnp.where(is_last, seed_state, incoming)

    top_state = lax.fori_loop(0, n_depth - 1, relay_step, seed_state)
    unused_state, deflection_bar = sweep(top_state)
    abar = deflection_bar.astype(jnp.bfloat16).reshape(planes_here, 2, blocks_here, width)
    contrib = jnp.einsum("pcbr,pbrk->pbck", abar, interp, preferred_element_type=jnp.float32)
    dest = dest_tile[:, :, 0]
    order_mask = jnp.arange(blocks_here)[None, :] < jnp.arange(blocks_here)[:, None]
    same_dest = dest[:, :, None] == dest[:, None, :]
    rank = jnp.sum(jnp.logical_and(same_dest, order_mask[None]), axis=2)
    slot = dest[0] * slots + rank[0]
    send_data = jnp.zeros((n_tile * slots, 2, width), jnp.float32).at[slot].set(contrib[0])
    send_ids = jnp.zeros((n_tile * slots,), jnp.int32).at[slot].set(dest_segment[0])
    got_data = lax.all_to_all(
        send_data.reshape(n_tile, slots, 2, width), "tile", split_axis=0, concat_axis=0, tiled=True
    )
    got_ids = lax.all_to_all(
        send_ids.reshape(n_tile, slots), "tile", split_axis=0, concat_axis=0, tiled=True
    )
    summed = (
        jnp.zeros((segments, 2, width), jnp.float32)
        .at[got_ids.reshape(-1)]
        .add(got_data.reshape(-1, 2, width))
    )
    plane_maps = [jnp.transpose(summed, (1, 0, 2)).reshape(2, ROWS, COLS)]
    maps = jnp.stack(plane_maps)
    ay_ext = padded_2(maps[:, 1], (("tile", 1),), 1)
    raw = column_part(maps[:, 0]) + 0.5 * (ay_ext[:, :-2, :] - ay_ext[:, 2:, :])
    raw_ext = padded_2(raw, (("tile", 1),), 1)
    rows_done = 0.25 * raw_ext[:, :-2, :] + 0.5 * raw_ext[:, 1:-1, :] + 0.25 * raw_ext[:, 2:, :]
    return smooth_cols(rows_done)


def solution(mesh):
    return jax.shard_map(
        per_device,
        mesh=mesh,
        in_specs=(
            P("depth", None, "tile"),
            P("depth"),
            P("depth"),
            P("tile"),
            P("depth", "tile", None),
            P("depth", "tile"),
            P("depth", "tile", None, None),
        ),
        out_specs=P("depth", "tile", None),
        check_vma=False,
    )
```

profile of v0, /device:TPU:103, one launch (start us, length us, event | category | flops | bytes accessed | tf_op | source)
XLA Modules:
  0.0 640.3 jit_solution(10379709504389961642)
XLA Ops:
  19.2 129.9 %all-reduce.4.cloned.1.call-done = f32[2,16384]{1,0:T(2,128)} async-done(((f32[2,16384]{1,0:T(2,128)}), f32[2,16384]{1,0:T(2,128)}) %all-reduce.4.cloned.1.call-update) | async-done | bytes 131088 | tf_op jit(solution)/shard_map/psum | solution.py:56
  151.7 387.7 %while.10 = (s32[]{:T(128)}, f32[4,16384]{1,0:T(4,128)S(1)}, pred[]{:T(512)}, f32[1,1,16384]{2,1,0:T(1,128)S(1)}, f32[1]{0:T(128)}, /*index=5*/f32[1,1,16384]{2,...) while((s32[]{:T(128)}, f32[4,16384]{1,0:T(4,128)S(1)}, pred[]{:T(512)}, ...), condition=%wide.region_4.5_spmd, body=%wide.region_3.4_spmd.sunk | while | flops 458754 | bytes 3342474 | solution.py:84
  166.8 8.5 %collective-permute-done = f32[4,16384]{1,0:T(4,128)S(1)} collective-permute-done((f32[4,16384]{1,0:T(4,128)S(1)}, f32[4,16384]{1,0:T(4,128)S(1)}, u32[]{:S(2)}, u32[]{:S(2)}) %collective-permute-start) | collective-permute-done | bytes 262176 | tf_op jit(solution)/shard_map/while/body/eval_jaxpr/ppermute | solution.py:13
  178.7 8.5 %collective-permute-done = f32[4,16384]{1,0:T(4,128)S(1)} collective-permute-done((f32[4,16384]{1,0:T(4,128)S(1)}, f32[4,16384]{1,0:T(4,128)S(1)}, u32[]{:S(2)}, u32[]{:S(2)}) %collective-permute-start) | collective-permute-done | bytes 262176 | tf_op jit(solution)/shard_map/while/body/eval_jaxpr/ppermute | solution.py:13
  190.5 8.5 %collective-permute-done = f32[4,16384]{1,0:T(4,128)S(1)} collective-permute-done((f32[4,16384]{1,0:T(4,128)S(1)}, f32[4,16384]{1,0:T(4,128)S(1)}, u32[]{:S(2)}, u32[]{:S(2)}) %collective-permute-start) | collective-permute-done | bytes 262176 | tf_op jit(solution)/shard_map/while/body/eval_jaxpr/ppermute | solution.py:13
  202.4 8.7 %collective-permute-done = f32[4,16384]{1,0:T(4,128)S(1)} collective-permute-done((f32[4,16384]{1,0:T(4,128)S(1)}, f32[4,16384]{1,0:T(4,128)S(1)}, u32[]{:S(2)}, u32[]{:S(2)}) %collective-permute-start) | collective-permute-done | bytes 262176 | tf_op jit(solution)/shard_map/while/body/eval_jaxpr/ppermute | solution.py:13
  214.5 9.9 %collective-permute-done = f32[4,16384]{1,0:T(4,128)S(1)} collective-permute-done((f32[4,16384]{1,0:T(4,128)S(1)}, f32[4,16384]{1,0:T(4,128)S(1)}, u32[]{:S(2)}, u32[]{:S(2)}) %collective-permute-start) | collective-permute-done | bytes 262176 | tf_op jit(solution)/shard_map/while/body/eval_jaxpr/ppermute | solution.py:13
  227.7 11.0 %collective-permute-done = f32[4,16384]{1,0:T(4,128)S(1)} collective-permute-done((f32[4,16384]{1,0:T(4,128)S(1)}, f32[4,16384]{1,0:T(4,128)S(1)}, u32[]{:S(2)}, u32[]{:S(2)}) %collective-permute-start) | collective-permute-done | bytes 262176 | tf_op jit(solution)/shard_map/while/body/eval_jaxpr/ppermute | solution.py:13
  242.0 10.8 %collective-permute-done = f32[4,16384]{1,0:T(4,128)S(1)} collective-permute-done((f32[4,16384]{1,0:T(4,128)S(1)}, f32[4,16384]{1,0:T(4,128)S(1)}, u32[]{:S(2)}, u32[]{:S(2)}) %collective-permute-start) | collective-permute-done | bytes 262176 | tf_op jit(solution)/shard_map/while/body/eval_jaxpr/ppermute | solution.py:13
  256.1 9.9 %collective-permute-done = f32[4,16384]{1,0:T(4,128)S(1)} collective-permute-done((f32[4,16384]{1,0:T(4,128)S(1)}, f32[4,16384]{1,0:T(4,128)S(1)}, u32[]{:S(2)}, u32[]{:S(2)}) %collective-permute-start) | collective-permute-done | bytes 262176 | tf_op jit(solution)/shard_map/while/body/eval_jaxpr/ppermute | solution.py:13
  269.4 9.1 %collective-permute-done = f32[4,16384]{1,0:T(4,128)S(1)} collective-permute-done((f32[4,16384]{1,0:T(4,128)S(1)}, f32[4,16384]{1,0:T(4,128)S(1)}, u32[]{:S(2)}, u32[]{:S(2)}) %collective-permute-start) | collective-permute-done | bytes 262176 | tf_op jit(solution)/shard_map/while/body/eval_jaxpr/ppermute | solution.py:13
  281.8 8.5 %collective-permute-done = f32[4,16384]{1,0:T(4,128)S(1)} collective-permute-done((f32[4,16384]{1,0:T(4,128)S(1)}, f32[4,16384]{1,0:T(4,128)S(1)}, u32[]{:S(2)}, u32[]{:S(2)}) %collective-permute-start) | collective-permute-done | bytes 262176 | tf_op jit(solution)/shard_map/while/body/eval_jaxpr/ppermute | solution.py:13
  293.7 8.5 %collective-permute-done = f32[4,16384]{1,0:T(4,128)S(1)} collective-permute-done((f32[4,16384]{1,0:T(4,128)S(1)}, f32[4,16384]{1,0:T(4,128)S(1)}, u32[]{:S(2)}, u32[]{:S(2)}) %collective-permute-start) | collective-permute-done | bytes 262176 | tf_op jit(solution)/shard_map/while/body/eval_jaxpr/ppermute | solution.py:13
  317.4 8.5 %collective-permute-done = f32[4,16384]{1,0:T(4,128)S(1)} collective-permute-done((f32[4,16384]{1,0:T(4,128)S(1)}, f32[4,16384]{1,0:T(4,128)S(1)}, u32[]{:S(2)}, u32[]{:S(2)}) %collective-permute-start) | collective-permute-done | bytes 262176 | tf_op jit(solution)/shard_map/while/body/eval_jaxpr/ppermute | solution.py:13
  329.3 8.5 %collective-permute-done = f32[4,16384]{1,0:T(4,128)S(1)} collective-permute-done((f32[4,16384]{1,0:T(4,128)S(1)}, f32[4,16384]{1,0:T(4,128)S(1)}, u32[]{:S(2)}, u32[]{:S(2)}) %collective-permute-start) | collective-permute-done | bytes 262176 | tf_op jit(solution)/shard_map/while/body/eval_jaxpr/ppermute | solution.py:13
  341.1 8.5 %collective-permute-done = f32[4,16384]{1,0:T(4,128)S(1)} collective-permute-done((f32[4,16384]{1,0:T(4,128)S(1)}, f32[4,16384]{1,0:T(4,128)S(1)}, u32[]{:S(2)}, u32[]{:S(2)}) %collective-permute-start) | collective-permute-done | bytes 262176 | tf_op jit(solution)/shard_map/while/body/eval_jaxpr/ppermute | solution.py:13
  353.0 8.6 %collective-permute-done = f32[4,16384]{1,0:T(4,128)S(1)} collective-permute-done((f32[4,16384]{1,0:T(4,128)S(1)}, f32[4,16384]{1,0:T(4,128)S(1)}, u32[]{:S(2)}, u32[]{:S(2)}) %collective-permute-start) | collective-permute-done | bytes 262176 | tf_op jit(solution)/shard_map/while/body/eval_jaxpr/ppermute | solution.py:13
  365.0 9.8 %collective-permute-done = f32[4,16384]{1,0:T(4,128)S(1)} collective-permute-done((f32[4,16384]{1,0:T(4,128)S(1)}, f32[4,16384]{1,0:T(4,128)S(1)}, u32[]{:S(2)}, u32[]{:S(2)}) %collective-permute-start) | collective-permute-done | bytes 262176 | tf_op jit(solution)/shard_map/while/body/eval_jaxpr/ppermute | solution.py:13
  378.1 10.9 %collective-permute-done = f32[4,16384]{1,0:T(4,128)S(1)} collective-permute-done((f32[4,16384]{1,0:T(4,128)S(1)}, f32[4,16384]{1,0:T(4,128)S(1)}, u32[]{:S(2)}, u32[]{:S(2)}) %collective-permute-start) | collective-permute-done | bytes 262176 | tf_op jit(solution)/shard_map/while/body/eval_jaxpr/ppermute | solution.py:13
  392.3 10.9 %collective-permute-done = f32[4,16384]{1,0:T(4,128)S(1)} collective-permute-done((f32[4,16384]{1,0:T(4,128)S(1)}, f32[4,16384]{1,0:T(4,128)S(1)}, u32[]{:S(2)}, u32[]{:S(2)}) %collective-permute-start) | collective-permute-done | bytes 262176 | tf_op jit(solution)/shard_map/while/body/eval_jaxpr/ppermute | solution.py:13
  406.6 10.0 %collective-permute-done = f32[4,16384]{1,0:T(4,128)S(1)} collective-permute-done((f32[4,16384]{1,0:T(4,128)S(1)}, f32[4,16384]{1,0:T(4,128)S(1)}, u32[]{:S(2)}, u32[]{:S(2)}) %collective-permute-start) | collective-permute-done | bytes 262176 | tf_op jit(solution)/shard_map/while/body/eval_jaxpr/ppermute | solution.py:13
  419.9 9.2 %collective-permute-done = f32[4,16384]{1,0:T(4,128)S(1)} collective-permute-done((f32[4,16384]{1,0:T(4,128)S(1)}, f32[4,16384]{1,0:T(4,128)S(1)}, u32[]{:S(2)}, u32[]{:S(2)}) %collective-permute-start) | collective-permute-done | bytes 262176 | tf_op jit(solution)/shard_map/while/body/eval_jaxpr/ppermute | solution.py:13
  432.5 8.5 %collective-permute-done = f32[4,16384]{1,0:T(4,128)S(1)} collective-permute-done((f32[4,16384]{1,0:T(4,128)S(1)}, f32[4,16384]{1,0:T(4,128)S(1)}, u32[]{:S(2)}, u32[]{:S(2)}) %collective-permute-start) | collective-permute-done | bytes 262176 | tf_op jit(solution)/shard_map/while/body/eval_jaxpr/ppermute | solution.py:13
  444.3 8.5 %collective-permute-done = f32[4,16384]{1,0:T(4,128)S(1)} collective-permute-done((f32[4,16384]{1,0:T(4,128)S(1)}, f32[4,16384]{1,0:T(4,128)S(1)}, u32[]{:S(2)}, u32[]{:S(2)}) %collective-permute-start) | collective-permute-done | bytes 262176 | tf_op jit(solution)/shard_map/while/body/eval_jaxpr/ppermute | solution.py:13
  456.2 8.5 %collective-permute-done = f32[4,16384]{1,0:T(4,128)S(1)} collective-permute-done((f32[4,16384]{1,0:T(4,128)S(1)}, f32[4,16384]{1,0:T(4,128)S(1)}, u32[]{:S(2)}, u32[]{:S(2)}) %collective-permute-start) | collective-permute-done | bytes 262176 | tf_op jit(solution)/shard_map/while/body/eval_jaxpr/ppermute | solution.py:13
  479.9 8.5 %collective-permute-done = f32[4,16384]{1,0:T(4,128)S(1)} collective-permute-done((f32[4,16384]{1,0:T(4,128)S(1)}, f32[4,16384]{1,0:T(4,128)S(1)}, u32[]{:S(2)}, u32[]{:S(2)}) %collective-permute-start) | collective-permute-done | bytes 262176 | tf_op jit(solution)/shard_map/while/body/eval_jaxpr/ppermute | solution.py:13
  491.8 8.5 %collective-permute-done = f32[4,16384]{1,0:T(4,128)S(1)} collective-permute-done((f32[4,16384]{1,0:T(4,128)S(1)}, f32[4,16384]{1,0:T(4,128)S(1)}, u32[]{:S(2)}, u32[]{:S(2)}) %collective-permute-start) | collective-permute-done | bytes 262176 | tf_op jit(solution)/shard_map/while/body/eval_jaxpr/ppermute | solution.py:13
  515.5 9.6 %collective-permute-done = f32[4,16384]{1,0:T(4,128)S(1)} collective-permute-done((f32[4,16384]{1,0:T(4,128)S(1)}, f32[4,16384]{1,0:T(4,128)S(1)}, u32[]{:S(2)}, u32[]{:S(2)}) %collective-permute-start) | collective-permute-done | bytes 262176 | tf_op jit(solution)/shard_map/while/body/eval_jaxpr/ppermute | solution.py:13
  528.5 10.8 %collective-permute-done = f32[4,16384]{1,0:T(4,128)S(1)} collective-permute-done((f32[4,16384]{1,0:T(4,128)S(1)}, f32[4,16384]{1,0:T(4,128)S(1)}, u32[]{:S(2)}, u32[]{:S(2)}) %collective-permute-start) | collective-permute-done | bytes 262176 | tf_op jit(solution)/shard_map/while/body/eval_jaxpr/ppermute | solution.py:13
  543.8 12.5 %scatter_fusion = f32[256,2,128]{2,1,0:T(2,128)} fusion(f32[256,2,128]{2,1,0:T(2,128)} %broadcast.154.clone, s32[128]{0:T(128)S(1)} %fusion.14, f32[128,2,128]{2,1,0:T(2,128)S(1)} %fusion.4), kind=kCustom, calls=%fused_computation.1 | custom fusion | bytes 393728 | tf_op jit(solution)/shard_map/scatter | solution.py:93
  556.2 43.4 %all-to-all-start.1 = ((f32[8,32,2,128]{3,2,1,0:T(2,128)}), f32[8,32,2,128]{3,2,1,0:T(2,128)S(1)}, u32[]{:S(2)}, u32[]{:S(2)}) async-start(f32[8,32,2,128]{3,2,1,0:T(2,128)} %bitcast.21), calls=%async_computation.1 | async-start | bytes 524288 | tf_op jit(solution)/shard_map/all_to_all | solution.py:95
  606.2 8.7 %scatter_fusion.1 = f32[256,2,128]{2,1,0:T(2,128)S(1)} fusion(f32[256,2,128]{2,1,0:T(2,128)S(1)} %broadcast.154, s32[256]{0:T(256)S(1)} %bitcast.85, f32[256,2,128]{2,1,0:T(2,128)S(1)} %bitcast.80), kind=kCustom, calls=%fused_computation.2 | custom fusion | flops 65536 | bytes 787456 | tf_op jit(solution)/shard_map/scatter-add | solution.py:104
  (201 shorter events, 179.8 us)
Async XLA Ops:
  6.5 142.5 %all-reduce.4.cloned.1.call-start = ((), (), s32[]{:S(2)}) async-start(), calls=%async_computation.2 | async-start | bytes 262144 | tf_op jit(solution)/shard_map/psum | solution.py:56
  12.4 543.8 %all-to-all-start = ((s32[8,1,32]{2,1,0:T(1,128)}), s32[8,1,32]{2,1,0:T(1,128)S(1)}, u32[]{:S(2)}, u32[]{:S(2)}) async-start(s32[8,1,32]{2,1,0:T(1,128)} %all_to_all.9), calls=%async_computation | async-start | bytes 8192 | tf_op jit(solution)/shard_map/all_to_all | solution.py:98
  153.0 10.4 %collective-permute-start = (f32[4,16384]{1,0:T(4,128)S(1)}, f32[4,16384]{1,0:T(4,128)S(1)}, u32[]{:S(2)}, u32[]{:S(2)}) collective-permute-start(f32[4,16384]{1,0:T(4,128)S(1)} %pad_maximum_fusion.7), channel_id=1, source_target_pairs={{8,0},{16,8},{24,16},{32,24},{40,32},{48,40},{56,48},{64,56},{72,6... | collective-permute-start | bytes 786440 | tf_op jit(solution)/shard_map/while/body/eval_jaxpr/ppermute | solution.py:13
  164.9 10.4 %collective-permute-start = (f32[4,16384]{1,0:T(4,128)S(1)}, f32[4,16384]{1,0:T(4,128)S(1)}, u32[]{:S(2)}, u32[]{:S(2)}) collective-permute-start(f32[4,16384]{1,0:T(4,128)S(1)} %pad_maximum_fusion.7), channel_id=1, source_target_pairs={{8,0},{16,8},{24,16},{32,24},{40,32},{48,40},{56,48},{64,56},{72,6... | collective-permute-start | bytes 786440 | tf_op jit(solution)/shard_map/while/body/eval_jaxpr/ppermute | solution.py:13
  176.7 10.4 %collective-permute-start = (f32[4,16384]{1,0:T(4,128)S(1)}, f32[4,16384]{1,0:T(4,128)S(1)}, u32[]{:S(2)}, u32[]{:S(2)}) collective-permute-start(f32[4,16384]{1,0:T(4,128)S(1)} %pad_maximum_fusion.7), channel_id=1, source_target_pairs={{8,0},{16,8},{24,16},{32,24},{40,32},{48,40},{56,48},{64,56},{72,6... | collective-permute-start | bytes 786440 | tf_op jit(solution)/shard_map/while/body/eval_jaxpr/ppermute | solution.py:13
  188.6 10.4 %collective-permute-start = (f32[4,16384]{1,0:T(4,128)S(1)}, f32[4,16384]{1,0:T(4,128)S(1)}, u32[]{:S(2)}, u32[]{:S(2)}) collective-permute-start(f32[4,16384]{1,0:T(4,128)S(1)} %pad_maximum_fusion.7), channel_id=1, source_target_pairs={{8,0},{16,8},{24,16},{32,24},{40,32},{48,40},{56,48},{64,56},{72,6... | collective-permute-start | bytes 786440 | tf_op jit(solution)/shard_map/while/body/eval_jaxpr/ppermute | solution.py:13
  200.5 10.6 %collective-permute-start = (f32[4,16384]{1,0:T(4,128)S(1)}, f32[4,16384]{1,0:T(4,128)S(1)}, u32[]{:S(2)}, u32[]{:S(2)}) collective-permute-start(f32[4,16384]{1,0:T(4,128)S(1)} %pad_maximum_fusion.7), channel_id=1, source_target_pairs={{8,0},{16,8},{24,16},{32,24},{40,32},{48,40},{56,48},{64,56},{72,6... | collective-permute-start | bytes 786440 | tf_op jit(solution)/shard_map/while/body/eval_jaxpr/ppermute | solution.py:13
  212.5 11.8 %collective-permute-start = (f32[4,16384]{1,0:T(4,128)S(1)}, f32[4,16384]{1,0:T(4,128)S(1)}, u32[]{:S(2)}, u32[]{:S(2)}) collective-permute-start(f32[4,16384]{1,0:T(4,128)S(1)} %pad_maximum_fusion.7), channel_id=1, source_target_pairs={{8,0},{16,8},{24,16},{32,24},{40,32},{48,40},{56,48},{64,56},{72,6... | collective-permute-start | bytes 786440 | tf_op jit(solution)/shard_map/while/body/eval_jaxpr/ppermute | solution.py:13
  225.7 12.9 %collective-permute-start = (f32[4,16384]{1,0:T(4,128)S(1)}, f32[4,16384]{1,0:T(4,128)S(1)}, u32[]{:S(2)}, u32[]{:S(2)}) collective-permute-start(f32[4,16384]{1,0:T(4,128)S(1)} %pad_maximum_fusion.7), channel_id=1, source_target_pairs={{8,0},{16,8},{24,16},{32,24},{40,32},{48,40},{56,48},{64,56},{72,6... | collective-permute-start | bytes 786440 | tf_op jit(solution)/shard_map/while/body/eval_jaxpr/ppermute | solution.py:13
  240.1 12.7 %collective-permute-start = (f32[4,16384]{1,0:T(4,128)S(1)}, f32[4,16384]{1,0:T(4,128)S(1)}, u32[]{:S(2)}, u32[]{:S(2)}) collective-permute-start(f32[4,16384]{1,0:T(4,128)S(1)} %pad_maximum_fusion.7), channel_id=1, source_target_pairs={{8,0},{16,8},{24,16},{32,24},{40,32},{48,40},{56,48},{64,56},{72,6... | collective-permute-start | bytes 786440 | tf_op jit(solution)/shard_map/while/body/eval_jaxpr/ppermute | solution.py:13
  254.2 11.9 %collective-permute-start = (f32[4,16384]{1,0:T(4,128)S(1)}, f32[4,16384]{1,0:T(4,128)S(1)}, u32[]{:S(2)}, u32[]{:S(2)}) collective-permute-start(f32[4,16384]{1,0:T(4,128)S(1)} %pad_maximum_fusion.7), channel_id=1, source_target_pairs={{8,0},{16,8},{24,16},{32,24},{40,32},{48,40},{56,48},{64,56},{72,6... | collective-permute-start | bytes 786440 | tf_op jit(solution)/shard_map/while/body/eval_jaxpr/ppermute | solution.py:13
  267.5 11.0 %collective-permute-start = (f32[4,16384]{1,0:T(4,128)S(1)}, f32[4,16384]{1,0:T(4,128)S(1)}, u32[]{:S(2)}, u32[]{:S(2)}) collective-permute-start(f32[4,16384]{1,0:T(4,128)S(1)} %pad_maximum_fusion.7), channel_id=1, source_target_pairs={{8,0},{16,8},{24,16},{32,24},{40,32},{48,40},{56,48},{64,56},{72,6... | collective-permute-start | bytes 786440 | tf_op jit(solution)/shard_map/while/body/eval_jaxpr/ppermute | solution.py:13
  279.9 10.4 %collective-permute-start = (f32[4,16384]{1,0:T(4,128)S(1)}, f32[4,16384]{1,0:T(4,128)S(1)}, u32[]{:S(2)}, u32[]{:S(2)}) collective-permute-start(f32[4,16384]{1,0:T(4,128)S(1)} %pad_maximum_fusion.7), channel_id=1, source_target_pairs={{8,0},{16,8},{24,16},{32,24},{40,32},{48,40},{56,48},{64,56},{72,6... | collective-permute-start | bytes 786440 | tf_op jit(solution)/shard_map/while/body/eval_jaxpr/ppermute | solution.py:13
  291.8 10.4 %collective-permute-start = (f32[4,16384]{1,0:T(4,128)S(1)}, f32[4,16384]{1,0:T(4,128)S(1)}, u32[]{:S(2)}, u32[]{:S(2)}) collective-permute-start(f32[4,16384]{1,0:T(4,128)S(1)} %pad_maximum_fusion.7), channel_id=1, source_target_pairs={{8,0},{16,8},{24,16},{32,24},{40,32},{48,40},{56,48},{64,56},{72,6... | collective-permute-start | bytes 786440 | tf_op jit(solution)/shard_map/while/body/eval_jaxpr/ppermute | solution.py:13
  303.6 10.4 %collective-permute-start = (f32[4,16384]{1,0:T(4,128)S(1)}, f32[4,16384]{1,0:T(4,128)S(1)}, u32[]{:S(2)}, u32[]{:S(2)}) collective-permute-start(f32[4,16384]{1,0:T(4,128)S(1)} %pad_maximum_fusion.7), channel_id=1, source_target_pairs={{8,0},{16,8},{24,16},{32,24},{40,32},{48,40},{56,48},{64,56},{72,6... | collective-permute-start | bytes 786440 | tf_op jit(solution)/shard_map/while/body/eval_jaxpr/ppermute | solution.py:13
  315.5 10.4 %collective-permute-start = (f32[4,16384]{1,0:T(4,128)S(1)}, f32[4,16384]{1,0:T(4,128)S(1)}, u32[]{:S(2)}, u32[]{:S(2)}) collective-permute-start(f32[4,16384]{1,0:T(4,128)S(1)} %pad_maximum_fusion.7), channel_id=1, source_target_pairs={{8,0},{16,8},{24,16},{32,24},{40,32},{48,40},{56,48},{64,56},{72,6... | collective-permute-start | bytes 786440 | tf_op jit(solution)/shard_map/while/body/eval_jaxpr/ppermute | solution.py:13
  327.4 10.4 %collective-permute-start = (f32[4,16384]{1,0:T(4,128)S(1)}, f32[4,16384]{1,0:T(4,128)S(1)}, u32[]{:S(2)}, u32[]{:S(2)}) collective-permute-start(f32[4,16384]{1,0:T(4,128)S(1)} %pad_maximum_fusion.7), channel_id=1, source_target_pairs={{8,0},{16,8},{24,16},{32,24},{40,32},{48,40},{56,48},{64,56},{72,6... | collective-permute-start | bytes 786440 | tf_op jit(solution)/shard_map/while/body/eval_jaxpr/ppermute | solution.py:13
  339.2 10.4 %collective-permute-start = (f32[4,16384]{1,0:T(4,128)S(1)}, f32[4,16384]{1,0:T(4,128)S(1)}, u32[]{:S(2)}, u32[]{:S(2)}) collective-permute-start(f32[4,16384]{1,0:T(4,128)S(1)} %pad_maximum_fusion.7), channel_id=1, source_target_pairs={{8,0},{16,8},{24,16},{32,24},{40,32},{48,40},{56,48},{64,56},{72,6... | collective-permute-start | bytes 786440 | tf_op jit(solution)/shard_map/while/body/eval_jaxpr/ppermute | solution.py:13
  351.1 10.5 %collective-permute-start = (f32[4,16384]{1,0:T(4,128)S(1)}, f32[4,16384]{1,0:T(4,128)S(1)}, u32[]{:S(2)}, u32[]{:S(2)}) collective-permute-start(f32[4,16384]{1,0:T(4,128)S(1)} %pad_maximum_fusion.7), channel_id=1, source_target_pairs={{8,0},{16,8},{24,16},{32,24},{40,32},{48,40},{56,48},{64,56},{72,6... | collective-permute-start | bytes 786440 | tf_op jit(solution)/shard_map/while/body/eval_jaxpr/ppermute | solution.py:13
  363.0 11.7 %collective-permute-start = (f32[4,16384]{1,0:T(4,128)S(1)}, f32[4,16384]{1,0:T(4,128)S(1)}, u32[]{:S(2)}, u32[]{:S(2)}) collective-permute-start(f32[4,16384]{1,0:T(4,128)S(1)} %pad_maximum_fusion.7), channel_id=1, source_target_pairs={{8,0},{16,8},{24,16},{32,24},{40,32},{48,40},{56,48},{64,56},{72,6... | collective-permute-start | bytes 786440 | tf_op jit(solution)/shard_map/while/body/eval_jaxpr/ppermute | solution.py:13
  376.1 12.8 %collective-permute-start = (f32[4,16384]{1,0:T(4,128)S(1)}, f32[4,16384]{1,0:T(4,128)S(1)}, u32[]{:S(2)}, u32[]{:S(2)}) collective-permute-start(f32[4,16384]{1,0:T(4,128)S(1)} %pad_maximum_fusion.7), channel_id=1, source_target_pairs={{8,0},{16,8},{24,16},{32,24},{40,32},{48,40},{56,48},{64,56},{72,6... | collective-permute-start | bytes 786440 | tf_op jit(solution)/shard_map/while/body/eval_jaxpr/ppermute | solution.py:13
  390.4 12.8 %collective-permute-start = (f32[4,16384]{1,0:T(4,128)S(1)}, f32[4,16384]{1,0:T(4,128)S(1)}, u32[]{:S(2)}, u32[]{:S(2)}) collective-permute-start(f32[4,16384]{1,0:T(4,128)S(1)} %pad_maximum_fusion.7), channel_id=1, source_target_pairs={{8,0},{16,8},{24,16},{32,24},{40,32},{48,40},{56,48},{64,56},{72,6... | collective-permute-start | bytes 786440 | tf_op jit(solution)/shard_map/while/body/eval_jaxpr/ppermute | solution.py:13
  404.6 12.0 %collective-permute-start = (f32[4,16384]{1,0:T(4,128)S(1)}, f32[4,16384]{1,0:T(4,128)S(1)}, u32[]{:S(2)}, u32[]{:S(2)}) collective-permute-start(f32[4,16384]{1,0:T(4,128)S(1)} %pad_maximum_fusion.7), channel_id=1, source_target_pairs={{8,0},{16,8},{24,16},{32,24},{40,32},{48,40},{56,48},{64,56},{72,6... | collective-permute-start | bytes 786440 | tf_op jit(solution)/shard_map/while/body/eval_jaxpr/ppermute | solution.py:13
  418.0 11.1 %collective-permute-start = (f32[4,16384]{1,0:T(4,128)S(1)}, f32[4,16384]{1,0:T(4,128)S(1)}, u32[]{:S(2)}, u32[]{:S(2)}) collective-permute-start(f32[4,16384]{1,0:T(4,128)S(1)} %pad_maximum_fusion.7), channel_id=1, source_target_pairs={{8,0},{16,8},{24,16},{32,24},{40,32},{48,40},{56,48},{64,56},{72,6... | collective-permute-start | bytes 786440 | tf_op jit(solution)/shard_map/while/body/eval_jaxpr/ppermute | solution.py:13
  430.5 10.4 %collective-permute-start = (f32[4,16384]{1,0:T(4,128)S(1)}, f32[4,16384]{1,0:T(4,128)S(1)}, u32[]{:S(2)}, u32[]{:S(2)}) collective-permute-start(f32[4,16384]{1,0:T(4,128)S(1)} %pad_maximum_fusion.7), channel_id=1, source_target_pairs={{8,0},{16,8},{24,16},{32,24},{40,32},{48,40},{56,48},{64,56},{72,6... | collective-permute-start | bytes 786440 | tf_op jit(solution)/shard_map/while/body/eval_jaxpr/ppermute | solution.py:13
  442.4 10.4 %collective-permute-start = (f32[4,16384]{1,0:T(4,128)S(1)}, f32[4,16384]{1,0:T(4,128)S(1)}, u32[]{:S(2)}, u32[]{:S(2)}) collective-permute-start(f32[4,16384]{1,0:T(4,128)S(1)} %pad_maximum_fusion.7), channel_id=1, source_target_pairs={{8,0},{16,8},{24,16},{32,24},{40,32},{48,40},{56,48},{64,56},{72,6... | collective-permute-start | bytes 786440 | tf_op jit(solution)/shard_map/while/body/eval_jaxpr/ppermute | solution.py:13
  454.3 10.4 %collective-permute-start = (f32[4,16384]{1,0:T(4,128)S(1)}, f32[4,16384]{1,0:T(4,128)S(1)}, u32[]{:S(2)}, u32[]{:S(2)}) collective-permute-start(f32[4,16384]{1,0:T(4,128)S(1)} %pad_maximum_fusion.7), channel_id=1, source_target_pairs={{8,0},{16,8},{24,16},{32,24},{40,32},{48,40},{56,48},{64,56},{72,6... | collective-permute-start | bytes 786440 | tf_op jit(solution)/shard_map/while/body/eval_jaxpr/ppermute | solution.py:13
  478.0 10.4 %collective-permute-start = (f32[4,16384]{1,0:T(4,128)S(1)}, f32[4,16384]{1,0:T(4,128)S(1)}, u32[]{:S(2)}, u32[]{:S(2)}) collective-permute-start(f32[4,16384]{1,0:T(4,128)S(1)} %pad_maximum_fusion.7), channel_id=1, source_target_pairs={{8,0},{16,8},{24,16},{32,24},{40,32},{48,40},{56,48},{64,56},{72,6... | collective-permute-start | bytes 786440 | tf_op jit(solution)/shard_map/while/body/eval_jaxpr/ppermute | solution.py:13
  489.8 10.4 %collective-permute-start = (f32[4,16384]{1,0:T(4,128)S(1)}, f32[4,16384]{1,0:T(4,128)S(1)}, u32[]{:S(2)}, u32[]{:S(2)}) collective-permute-start(f32[4,16384]{1,0:T(4,128)S(1)} %pad_maximum_fusion.7), channel_id=1, source_target_pairs={{8,0},{16,8},{24,16},{32,24},{40,32},{48,40},{56,48},{64,56},{72,6... | collective-permute-start | bytes 786440 | tf_op jit(solution)/shard_map/while/body/eval_jaxpr/ppermute | solution.py:13
  513.6 11.6 %collective-permute-start = (f32[4,16384]{1,0:T(4,128)S(1)}, f32[4,16384]{1,0:T(4,128)S(1)}, u32[]{:S(2)}, u32[]{:S(2)}) collective-permute-start(f32[4,16384]{1,0:T(4,128)S(1)} %pad_maximum_fusion.7), channel_id=1, source_target_pairs={{8,0},{16,8},{24,16},{32,24},{40,32},{48,40},{56,48},{64,56},{72,6... | collective-permute-start | bytes 786440 | tf_op jit(solution)/shard_map/while/body/eval_jaxpr/ppermute | solution.py:13
  526.6 12.7 %collective-permute-start = (f32[4,16384]{1,0:T(4,128)S(1)}, f32[4,16384]{1,0:T(4,128)S(1)}, u32[]{:S(2)}, u32[]{:S(2)}) collective-permute-start(f32[4,16384]{1,0:T(4,128)S(1)} %pad_maximum_fusion.7), channel_id=1, source_target_pairs={{8,0},{16,8},{24,16},{32,24},{40,32},{48,40},{56,48},{64,56},{72,6... | collective-permute-start | bytes 786440 | tf_op jit(solution)/shard_map/while/body/eval_jaxpr/ppermute | solution.py:13
  556.2 49.9 %all-to-all-start.1 = ((f32[8,32,2,128]{3,2,1,0:T(2,128)}), f32[8,32,2,128]{3,2,1,0:T(2,128)S(1)}, u32[]{:S(2)}, u32[]{:S(2)}) async-start(f32[8,32,2,128]{3,2,1,0:T(2,128)} %bitcast.21), calls=%async_computation.1 | async-start | bytes 524288 | tf_op jit(solution)/shard_map/all_to_all | solution.py:95
  (6 other events, 41.7 us)
Sparse Core Ops, SparseCore 0:
  10.8 138.2 all-reduce.3
where the time goes:
time: 642 us; the launch traced here: 640 us
  waiting for transfers between devices  425 us (66%)
  starting transfers between devices  119 us (19%)
  other arithmetic  60.1 us (9%)
  local copies, waits for them, and re-layouts  17.1 us (3%)
  between operations  14.9 us (2%)
    ppermute x31, waiting for transfers between devices, from_behind(): lax.ppermute(value, axis, [(source, source + steps) for source in range(l...  283 us
    psum x1, waiting for transfers between devices, per_device(): shear = lax.psum(local_terms, 'depth')  130 us
    ppermute x31, starting transfers between devices, from_behind(): lax.ppermute(value, axis, [(source, source + steps) for source in range(l...  60.4 us
    all_to_all x1, starting transfers between devices, per_device(): lax.all_to_all(send_data.reshape(n_tile, slots, 2, width), 'tile', split_...  43.4 us
    sub x31, other arithmetic, sweep(): new_one = xb_one - (jxx[0] * tp_one + jxy[0] * tp_two)  27.6 us
  transfers between devices with their start and end apart: 38, of which 35 were waited for; matrix products, arithmetic and copies ran while one was open for 11% of the time, Pallas kernels for 0%

commit v1 on v0

--- a/solution.py
+++ b/solution.py
@@ -37,6 +37,22 @@
 
 
 def per_device(tidal, plane_weight, plane_step, ray_angle, dest_tile, dest_segment, interp):
+
+    def _treat_waves(sample, ax_name):
+        n_peers_all = jax.lax.axis_size(ax_name)
+
+        def mark_slabs(current_arr, main):
+            if main >= n_peers_all:
+                return current_arr
+            now = jax.lax.ppermute(
+                current_arr, ax_name, perm=[(rr, rr ^ main) for rr in range(n_peers_all)]
+            )
+            x_now = mark_slabs(current_arr + now, 2 * main)
+            return x_now
+
+        new = mark_slabs(sample, 1)
+        return new
+
     planes_here = tidal.shape[0]
     n_tile = lax.axis_size("tile")
     n_depth = lax.axis_size("depth")
@@ -53,7 +69,7 @@
             -jnp.sum(plane_weight[:, None] * jxy, axis=0),
         ]
     )
-    shear = lax.psum(local_terms, "depth")
+    shear = _treat_waves(local_terms, "depth")
     cross = -shear[0] * jnp.sin(2.0 * ray_angle) + shear[1] * jnp.cos(2.0 * ray_angle)
     seed_state = jnp.stack(
         [

time: 642 us -> 516 us (0.80)
  waiting for transfers between devices: 425 us -> 309 us
  between operations: 14.9 us -> 1.53 us
    psum x1 -> x0, waiting for transfers between devices: 130 us -> none  [per_device(): shear = lax.psum(local_terms, 'depth')]
    ppermute x0 -> x5, waiting for transfers between devices: none -> 13 us  [mark_slabs(): jax.lax.ppermute(current_arr, ax_name, perm=[(rr, rr ^ main) for rr in ra...]
    ppermute x0 -> x5, starting transfers between devices: none -> 7.88 us  [mark_slabs(): jax.lax.ppermute(current_arr, ax_name, perm=[(rr, rr ^ main) for rr in ra...]
  transfers between devices with their start and end apart: 38 -> 42, of which waited for: 35 -> 38; matrix products, arithmetic and copies ran while one was open for 11% -> 13% of each run, Pallas kernels for 0% -> 0%
where the time goes in v1:
time: 516 us; the launch traced here: 514 us
  waiting for transfers between devices  309 us (60%)
  starting transfers between devices  123 us (24%)
  other arithmetic  59 us (11%)
  local copies, waits for them, and re-layouts  17.1 us (3%)
    ppermute x31, waiting for transfers between devices, from_behind(): lax.ppermute(value, axis, [(source, source + steps) for source in range(l...  284 us
    ppermute x31, starting transfers between devices, from_behind(): lax.ppermute(value, axis, [(source, source + steps) for source in range(l...  60.1 us
    all_to_all x1, starting transfers between devices, per_device(): lax.all_to_all(send_data.reshape(n_tile, slots, 2, width), 'tile', split_...  37.3 us
    sub x31, other arithmetic, sweep(): new_one = xb_one - (jxx[0] * tp_one + jxy[0] * tp_two)  27.6 us
    ppermute x5, waiting for transfers between devices, mark_slabs(): jax.lax.ppermute(current_arr, ax_name, perm=[(rr, rr ^ main) for rr in ra...  13 us
    scatter x1, local copies, waits for them, and re-layouts, per_device(): jnp.zeros((n_tile * slots, 2, width), jnp.float32).at[slot].set(contrib[0])  12.5 us
  transfers between devices with their start and end apart: 42, of which 38 were waited for; matrix products, arithmetic and copies ran while one was open for 13% of the time, Pallas kernels for 0%

profile of v1, /device:TPU:103, one launch (start us, length us, event | category | flops | bytes accessed | tf_op | source)
XLA Modules:
  0.0 514.2 jit_solution(17493445885441464760)
XLA Ops:
  38.2 388.0 %while.10 = (s32[]{:T(128)}, f32[4,16384]{1,0:T(4,128)S(1)}, pred[]{:T(512)}, f32[1,1,16384]{2,1,0:T(1,128)S(1)}, f32[1]{0:T(128)}, /*index=5*/f32[1,1,16384]{2,...) while((s32[]{:T(128)}, f32[4,16384]{1,0:T(4,128)S(1)}, pred[]{:T(512)}, ...), condition=%wide.region_3.4_spmd, body=%wide.region_2.3_spmd.sunk | while | flops 458754 | bytes 3342474 | solution.py:100
  42.0 9.8 %collective-permute-done = f32[4,16384]{1,0:T(4,128)S(1)} collective-permute-done((f32[4,16384]{1,0:T(4,128)S(1)}, f32[4,16384]{1,0:T(4,128)S(1)}, u32[]{:S(2)}, u32[]{:S(2)}) %collective-permute-start) | collective-permute-done | bytes 262176 | tf_op jit(solution)/shard_map/while/body/eval_jaxpr/ppermute | solution.py:13
  55.1 9.5 %collective-permute-done = f32[4,16384]{1,0:T(4,128)S(1)} collective-permute-done((f32[4,16384]{1,0:T(4,128)S(1)}, f32[4,16384]{1,0:T(4,128)S(1)}, u32[]{:S(2)}, u32[]{:S(2)}) %collective-permute-start) | collective-permute-done | bytes 262176 | tf_op jit(solution)/shard_map/while/body/eval_jaxpr/ppermute | solution.py:13
  67.9 8.5 %collective-permute-done = f32[4,16384]{1,0:T(4,128)S(1)} collective-permute-done((f32[4,16384]{1,0:T(4,128)S(1)}, f32[4,16384]{1,0:T(4,128)S(1)}, u32[]{:S(2)}, u32[]{:S(2)}) %collective-permute-start) | collective-permute-done | bytes 262176 | tf_op jit(solution)/shard_map/while/body/eval_jaxpr/ppermute | solution.py:13
  79.8 8.5 %collective-permute-done = f32[4,16384]{1,0:T(4,128)S(1)} collective-permute-done((f32[4,16384]{1,0:T(4,128)S(1)}, f32[4,16384]{1,0:T(4,128)S(1)}, u32[]{:S(2)}, u32[]{:S(2)}) %collective-permute-start) | collective-permute-done | bytes 262176 | tf_op jit(solution)/shard_map/while/body/eval_jaxpr/ppermute | solution.py:13
  91.6 8.5 %collective-permute-done = f32[4,16384]{1,0:T(4,128)S(1)} collective-permute-done((f32[4,16384]{1,0:T(4,128)S(1)}, f32[4,16384]{1,0:T(4,128)S(1)}, u32[]{:S(2)}, u32[]{:S(2)}) %collective-permute-start) | collective-permute-done | bytes 262176 | tf_op jit(solution)/shard_map/while/body/eval_jaxpr/ppermute | solution.py:13
  103.5 8.5 %collective-permute-done = f32[4,16384]{1,0:T(4,128)S(1)} collective-permute-done((f32[4,16384]{1,0:T(4,128)S(1)}, f32[4,16384]{1,0:T(4,128)S(1)}, u32[]{:S(2)}, u32[]{:S(2)}) %collective-permute-start) | collective-permute-done | bytes 262176 | tf_op jit(solution)/shard_map/while/body/eval_jaxpr/ppermute | solution.py:13
  115.4 8.5 %collective-permute-done = f32[4,16384]{1,0:T(4,128)S(1)} collective-permute-done((f32[4,16384]{1,0:T(4,128)S(1)}, f32[4,16384]{1,0:T(4,128)S(1)}, u32[]{:S(2)}, u32[]{:S(2)}) %collective-permute-start) | collective-permute-done | bytes 262176 | tf_op jit(solution)/shard_map/while/body/eval_jaxpr/ppermute | solution.py:13
  127.2 8.5 %collective-permute-done = f32[4,16384]{1,0:T(4,128)S(1)} collective-permute-done((f32[4,16384]{1,0:T(4,128)S(1)}, f32[4,16384]{1,0:T(4,128)S(1)}, u32[]{:S(2)}, u32[]{:S(2)}) %collective-permute-start) | collective-permute-done | bytes 262176 | tf_op jit(solution)/shard_map/while/body/eval_jaxpr/ppermute | solution.py:13
  139.1 8.5 %collective-permute-done = f32[4,16384]{1,0:T(4,128)S(1)} collective-permute-done((f32[4,16384]{1,0:T(4,128)S(1)}, f32[4,16384]{1,0:T(4,128)S(1)}, u32[]{:S(2)}, u32[]{:S(2)}) %collective-permute-start) | collective-permute-done | bytes 262176 | tf_op jit(solution)/shard_map/while/body/eval_jaxpr/ppermute | solution.py:13
  150.9 9.4 %collective-permute-done = f32[4,16384]{1,0:T(4,128)S(1)} collective-permute-done((f32[4,16384]{1,0:T(4,128)S(1)}, f32[4,16384]{1,0:T(4,128)S(1)}, u32[]{:S(2)}, u32[]{:S(2)}) %collective-permute-start) | collective-permute-done | bytes 262176 | tf_op jit(solution)/shard_map/while/body/eval_jaxpr/ppermute | solution.py:13
  163.7 10.5 %collective-permute-done = f32[4,16384]{1,0:T(4,128)S(1)} collective-permute-done((f32[4,16384]{1,0:T(4,128)S(1)}, f32[4,16384]{1,0:T(4,128)S(1)}, u32[]{:S(2)}, u32[]{:S(2)}) %collective-permute-start) | collective-permute-done | bytes 262176 | tf_op jit(solution)/shard_map/while/body/eval_jaxpr/ppermute | solution.py:13
  177.5 11.3 %collective-permute-done = f32[4,16384]{1,0:T(4,128)S(1)} collective-permute-done((f32[4,16384]{1,0:T(4,128)S(1)}, f32[4,16384]{1,0:T(4,128)S(1)}, u32[]{:S(2)}, u32[]{:S(2)}) %collective-permute-start) | collective-permute-done | bytes 262176 | tf_op jit(solution)/shard_map/while/body/eval_jaxpr/ppermute | solution.py:13
  192.1 10.4 %collective-permute-done = f32[4,16384]{1,0:T(4,128)S(1)} collective-permute-done((f32[4,16384]{1,0:T(4,128)S(1)}, f32[4,16384]{1,0:T(4,128)S(1)}, u32[]{:S(2)}, u32[]{:S(2)}) %collective-permute-start) | collective-permute-done | bytes 262176 | tf_op jit(solution)/shard_map/while/body/eval_jaxpr/ppermute | solution.py:13
  205.9 9.6 %collective-permute-done = f32[4,16384]{1,0:T(4,128)S(1)} collective-permute-done((f32[4,16384]{1,0:T(4,128)S(1)}, f32[4,16384]{1,0:T(4,128)S(1)}, u32[]{:S(2)}, u32[]{:S(2)}) %collective-permute-start) | collective-permute-done | bytes 262176 | tf_op jit(solution)/shard_map/while/body/eval_jaxpr/ppermute | solution.py:13
  230.7 8.5 %collective-permute-done = f32[4,16384]{1,0:T(4,128)S(1)} collective-permute-done((f32[4,16384]{1,0:T(4,128)S(1)}, f32[4,16384]{1,0:T(4,128)S(1)}, u32[]{:S(2)}, u32[]{:S(2)}) %collective-permute-start) | collective-permute-done | bytes 262176 | tf_op jit(solution)/shard_map/while/body/eval_jaxpr/ppermute | solution.py:13
  242.5 8.5 %collective-permute-done = f32[4,16384]{1,0:T(4,128)S(1)} collective-permute-done((f32[4,16384]{1,0:T(4,128)S(1)}, f32[4,16384]{1,0:T(4,128)S(1)}, u32[]{:S(2)}, u32[]{:S(2)}) %collective-permute-start) | collective-permute-done | bytes 262176 | tf_op jit(solution)/shard_map/while/body/eval_jaxpr/ppermute | solution.py:13
  266.3 8.5 %collective-permute-done = f32[4,16384]{1,0:T(4,128)S(1)} collective-permute-done((f32[4,16384]{1,0:T(4,128)S(1)}, f32[4,16384]{1,0:T(4,128)S(1)}, u32[]{:S(2)}, u32[]{:S(2)}) %collective-permute-start) | collective-permute-done | bytes 262176 | tf_op jit(solution)/shard_map/while/body/eval_jaxpr/ppermute | solution.py:13
  278.1 8.5 %collective-permute-done = f32[4,16384]{1,0:T(4,128)S(1)} collective-permute-done((f32[4,16384]{1,0:T(4,128)S(1)}, f32[4,16384]{1,0:T(4,128)S(1)}, u32[]{:S(2)}, u32[]{:S(2)}) %collective-permute-start) | collective-permute-done | bytes 262176 | tf_op jit(solution)/shard_map/while/body/eval_jaxpr/ppermute | solution.py:13
  301.8 9.3 %collective-permute-done = f32[4,16384]{1,0:T(4,128)S(1)} collective-permute-done((f32[4,16384]{1,0:T(4,128)S(1)}, f32[4,16384]{1,0:T(4,128)S(1)}, u32[]{:S(2)}, u32[]{:S(2)}) %collective-permute-start) | collective-permute-done | bytes 262176 | tf_op jit(solution)/shard_map/while/body/eval_jaxpr/ppermute | solution.py:13
  314.5 10.4 %collective-permute-done = f32[4,16384]{1,0:T(4,128)S(1)} collective-permute-done((f32[4,16384]{1,0:T(4,128)S(1)}, f32[4,16384]{1,0:T(4,128)S(1)}, u32[]{:S(2)}, u32[]{:S(2)}) %collective-permute-start) | collective-permute-done | bytes 262176 | tf_op jit(solution)/shard_map/while/body/eval_jaxpr/ppermute | solution.py:13
  328.2 11.4 %collective-permute-done = f32[4,16384]{1,0:T(4,128)S(1)} collective-permute-done((f32[4,16384]{1,0:T(4,128)S(1)}, f32[4,16384]{1,0:T(4,128)S(1)}, u32[]{:S(2)}, u32[]{:S(2)}) %collective-permute-start) | collective-permute-done | bytes 262176 | tf_op jit(solution)/shard_map/while/body/eval_jaxpr/ppermute | solution.py:13
  342.9 10.5 %collective-permute-done = f32[4,16384]{1,0:T(4,128)S(1)} collective-permute-done((f32[4,16384]{1,0:T(4,128)S(1)}, f32[4,16384]{1,0:T(4,128)S(1)}, u32[]{:S(2)}, u32[]{:S(2)}) %collective-permute-start) | collective-permute-done | bytes 262176 | tf_op jit(solution)/shard_map/while/body/eval_jaxpr/ppermute | solution.py:13
  356.8 9.7 %collective-permute-done = f32[4,16384]{1,0:T(4,128)S(1)} collective-permute-done((f32[4,16384]{1,0:T(4,128)S(1)}, f32[4,16384]{1,0:T(4,128)S(1)}, u32[]{:S(2)}, u32[]{:S(2)}) %collective-permute-start) | collective-permute-done | bytes 262176 | tf_op jit(solution)/shard_map/while/body/eval_jaxpr/ppermute | solution.py:13
  369.8 8.8 %collective-permute-done = f32[4,16384]{1,0:T(4,128)S(1)} collective-permute-done((f32[4,16384]{1,0:T(4,128)S(1)}, f32[4,16384]{1,0:T(4,128)S(1)}, u32[]{:S(2)}, u32[]{:S(2)}) %collective-permute-start) | collective-permute-done | bytes 262176 | tf_op jit(solution)/shard_map/while/body/eval_jaxpr/ppermute | solution.py:13
  382.0 8.5 %collective-permute-done = f32[4,16384]{1,0:T(4,128)S(1)} collective-permute-done((f32[4,16384]{1,0:T(4,128)S(1)}, f32[4,16384]{1,0:T(4,128)S(1)}, u32[]{:S(2)}, u32[]{:S(2)}) %collective-permute-start) | collective-permute-done | bytes 262176 | tf_op jit(solution)/shard_map/while/body/eval_jaxpr/ppermute | solution.py:13
  393.9 8.5 %collective-permute-done = f32[4,16384]{1,0:T(4,128)S(1)} collective-permute-done((f32[4,16384]{1,0:T(4,128)S(1)}, f32[4,16384]{1,0:T(4,128)S(1)}, u32[]{:S(2)}, u32[]{:S(2)}) %collective-permute-start) | collective-permute-done | bytes 262176 | tf_op jit(solution)/shard_map/while/body/eval_jaxpr/ppermute | solution.py:13
  405.7 8.5 %collective-permute-done = f32[4,16384]{1,0:T(4,128)S(1)} collective-permute-done((f32[4,16384]{1,0:T(4,128)S(1)}, f32[4,16384]{1,0:T(4,128)S(1)}, u32[]{:S(2)}, u32[]{:S(2)}) %collective-permute-start) | collective-permute-done | bytes 262176 | tf_op jit(solution)/shard_map/while/body/eval_jaxpr/ppermute | solution.py:13
  417.6 8.5 %collective-permute-done = f32[4,16384]{1,0:T(4,128)S(1)} collective-permute-done((f32[4,16384]{1,0:T(4,128)S(1)}, f32[4,16384]{1,0:T(4,128)S(1)}, u32[]{:S(2)}, u32[]{:S(2)}) %collective-permute-start) | collective-permute-done | bytes 262176 | tf_op jit(solution)/shard_map/while/body/eval_jaxpr/ppermute | solution.py:13
  430.6 12.5 %scatter_fusion = f32[256,2,128]{2,1,0:T(2,128)} fusion(f32[256,2,128]{2,1,0:T(2,128)} %broadcast.154.clone, s32[128]{0:T(128)S(1)} %fusion.14, f32[128,2,128]{2,1,0:T(2,128)S(1)} %fusion.4), kind=kCustom, calls=%fused_computation.1 | custom fusion | bytes 393728 | tf_op jit(solution)/shard_map/scatter | solution.py:109
  443.1 37.3 %all-to-all-start.1 = ((f32[8,32,2,128]{3,2,1,0:T(2,128)}), f32[8,32,2,128]{3,2,1,0:T(2,128)S(1)}, u32[]{:S(2)}, u32[]{:S(2)}) async-start(f32[8,32,2,128]{3,2,1,0:T(2,128)} %bitcast.21), calls=%async_computation.1 | async-start | bytes 524288 | tf_op jit(solution)/shard_map/all_to_all | solution.py:111
  486.9 8.7 %scatter_fusion.1 = f32[256,2,128]{2,1,0:T(2,128)S(1)} fusion(f32[256,2,128]{2,1,0:T(2,128)S(1)} %broadcast.154, s32[256]{0:T(256)S(1)} %bitcast.85, f32[256,2,128]{2,1,0:T(2,128)S(1)} %bitcast.80), kind=kCustom, calls=%fused_computation.2 | custom fusion | flops 65536 | bytes 787456 | tf_op jit(solution)/shard_map/scatter-add | solution.py:120
  (213 shorter events, 194.7 us)
Async XLA Ops:
  16.0 10.9 %collective-permute-start.4 = (f32[2,16384]{1,0:T(2,128)S(1)}, f32[2,16384]{1,0:T(2,128)S(1)}, u32[]{:S(2)}, u32[]{:S(2)}) collective-permute-start(f32[2,16384]{1,0:T(2,128)S(1)} %add.113), channel_id=1, source_target_pairs={{0,64},{8,72},{16,80},{24,88},{32,96},{40,104},{48,112},{56,120},{... | collective-permute-start | bytes 393224 | tf_op jit(solution)/shard_map/ppermute | solution.py:47
  18.6 424.5 %all-to-all-start = ((s32[8,1,32]{2,1,0:T(1,128)}), s32[8,1,32]{2,1,0:T(1,128)S(1)}, u32[]{:S(2)}, u32[]{:S(2)}) async-start(s32[8,1,32]{2,1,0:T(1,128)} %all_to_all.9), calls=%async_computation | async-start | bytes 8192 | tf_op jit(solution)/shard_map/all_to_all | solution.py:114
  39.5 12.2 %collective-permute-start = (f32[4,16384]{1,0:T(4,128)S(1)}, f32[4,16384]{1,0:T(4,128)S(1)}, u32[]{:S(2)}, u32[]{:S(2)}) collective-permute-start(f32[4,16384]{1,0:T(4,128)S(1)} %pad_maximum_fusion.7), channel_id=1, source_target_pairs={{8,0},{16,8},{24,16},{32,24},{40,32},{48,40},{56,48},{64,56},{72,6... | collective-permute-start | bytes 786440 | tf_op jit(solution)/shard_map/while/body/eval_jaxpr/ppermute | solution.py:13
  53.2 11.4 %collective-permute-start = (f32[4,16384]{1,0:T(4,128)S(1)}, f32[4,16384]{1,0:T(4,128)S(1)}, u32[]{:S(2)}, u32[]{:S(2)}) collective-permute-start(f32[4,16384]{1,0:T(4,128)S(1)} %pad_maximum_fusion.7), channel_id=1, source_target_pairs={{8,0},{16,8},{24,16},{32,24},{40,32},{48,40},{56,48},{64,56},{72,6... | collective-permute-start | bytes 786440 | tf_op jit(solution)/shard_map/while/body/eval_jaxpr/ppermute | solution.py:13
  66.0 10.4 %collective-permute-start = (f32[4,16384]{1,0:T(4,128)S(1)}, f32[4,16384]{1,0:T(4,128)S(1)}, u32[]{:S(2)}, u32[]{:S(2)}) collective-permute-start(f32[4,16384]{1,0:T(4,128)S(1)} %pad_maximum_fusion.7), channel_id=1, source_target_pairs={{8,0},{16,8},{24,16},{32,24},{40,32},{48,40},{56,48},{64,56},{72,6... | collective-permute-start | bytes 786440 | tf_op jit(solution)/shard_map/while/body/eval_jaxpr/ppermute | solution.py:13
  77.8 10.4 %collective-permute-start = (f32[4,16384]{1,0:T(4,128)S(1)}, f32[4,16384]{1,0:T(4,128)S(1)}, u32[]{:S(2)}, u32[]{:S(2)}) collective-permute-start(f32[4,16384]{1,0:T(4,128)S(1)} %pad_maximum_fusion.7), channel_id=1, source_target_pairs={{8,0},{16,8},{24,16},{32,24},{40,32},{48,40},{56,48},{64,56},{72,6... | collective-permute-start | bytes 786440 | tf_op jit(solution)/shard_map/while/body/eval_jaxpr/ppermute | solution.py:13
  89.7 10.4 %collective-permute-start = (f32[4,16384]{1,0:T(4,128)S(1)}, f32[4,16384]{1,0:T(4,128)S(1)}, u32[]{:S(2)}, u32[]{:S(2)}) collective-permute-start(f32[4,16384]{1,0:T(4,128)S(1)} %pad_maximum_fusion.7), channel_id=1, source_target_pairs={{8,0},{16,8},{24,16},{32,24},{40,32},{48,40},{56,48},{64,56},{72,6... | collective-permute-start | bytes 786440 | tf_op jit(solution)/shard_map/while/body/eval_jaxpr/ppermute | solution.py:13
  101.6 10.4 %collective-permute-start = (f32[4,16384]{1,0:T(4,128)S(1)}, f32[4,16384]{1,0:T(4,128)S(1)}, u32[]{:S(2)}, u32[]{:S(2)}) collective-permute-start(f32[4,16384]{1,0:T(4,128)S(1)} %pad_maximum_fusion.7), channel_id=1, source_target_pairs={{8,0},{16,8},{24,16},{32,24},{40,32},{48,40},{56,48},{64,56},{72,6... | collective-permute-start | bytes 786440 | tf_op jit(solution)/shard_map/while/body/eval_jaxpr/ppermute | solution.py:13
  113.4 10.4 %collective-permute-start = (f32[4,16384]{1,0:T(4,128)S(1)}, f32[4,16384]{1,0:T(4,128)S(1)}, u32[]{:S(2)}, u32[]{:S(2)}) collective-permute-start(f32[4,16384]{1,0:T(4,128)S(1)} %pad_maximum_fusion.7), channel_id=1, source_target_pairs={{8,0},{16,8},{24,16},{32,24},{40,32},{48,40},{56,48},{64,56},{72,6... | collective-permute-start | bytes 786440 | tf_op jit(solution)/shard_map/while/body/eval_jaxpr/ppermute | solution.py:13
  125.3 10.4 %collective-permute-start = (f32[4,16384]{1,0:T(4,128)S(1)}, f32[4,16384]{1,0:T(4,128)S(1)}, u32[]{:S(2)}, u32[]{:S(2)}) collective-permute-start(f32[4,16384]{1,0:T(4,128)S(1)} %pad_maximum_fusion.7), channel_id=1, source_target_pairs={{8,0},{16,8},{24,16},{32,24},{40,32},{48,40},{56,48},{64,56},{72,6... | collective-permute-start | bytes 786440 | tf_op jit(solution)/shard_map/while/body/eval_jaxpr/ppermute | solution.py:13
  137.1 10.4 %collective-permute-start = (f32[4,16384]{1,0:T(4,128)S(1)}, f32[4,16384]{1,0:T(4,128)S(1)}, u32[]{:S(2)}, u32[]{:S(2)}) collective-permute-start(f32[4,16384]{1,0:T(4,128)S(1)} %pad_maximum_fusion.7), channel_id=1, source_target_pairs={{8,0},{16,8},{24,16},{32,24},{40,32},{48,40},{56,48},{64,56},{72,6... | collective-permute-start | bytes 786440 | tf_op jit(solution)/shard_map/while/body/eval_jaxpr/ppermute | solution.py:13
  149.0 11.3 %collective-permute-start = (f32[4,16384]{1,0:T(4,128)S(1)}, f32[4,16384]{1,0:T(4,128)S(1)}, u32[]{:S(2)}, u32[]{:S(2)}) collective-permute-start(f32[4,16384]{1,0:T(4,128)S(1)} %pad_maximum_fusion.7), channel_id=1, source_target_pairs={{8,0},{16,8},{24,16},{32,24},{40,32},{48,40},{56,48},{64,56},{72,6... | collective-permute-start | bytes 786440 | tf_op jit(solution)/shard_map/while/body/eval_jaxpr/ppermute | solution.py:13
  161.7 12.4 %collective-permute-start = (f32[4,16384]{1,0:T(4,128)S(1)}, f32[4,16384]{1,0:T(4,128)S(1)}, u32[]{:S(2)}, u32[]{:S(2)}) collective-permute-start(f32[4,16384]{1,0:T(4,128)S(1)} %pad_maximum_fusion.7), channel_id=1, source_target_pairs={{8,0},{16,8},{24,16},{32,24},{40,32},{48,40},{56,48},{64,56},{72,6... | collective-permute-start | bytes 786440 | tf_op jit(solution)/shard_map/while/body/eval_jaxpr/ppermute | solution.py:13
  175.6 13.2 %collective-permute-start = (f32[4,16384]{1,0:T(4,128)S(1)}, f32[4,16384]{1,0:T(4,128)S(1)}, u32[]{:S(2)}, u32[]{:S(2)}) collective-permute-start(f32[4,16384]{1,0:T(4,128)S(1)} %pad_maximum_fusion.7), channel_id=1, source_target_pairs={{8,0},{16,8},{24,16},{32,24},{40,32},{48,40},{56,48},{64,56},{72,6... | collective-permute-start | bytes 786440 | tf_op jit(solution)/shard_map/while/body/eval_jaxpr/ppermute | solution.py:13
  190.2 12.3 %collective-permute-start = (f32[4,16384]{1,0:T(4,128)S(1)}, f32[4,16384]{1,0:T(4,128)S(1)}, u32[]{:S(2)}, u32[]{:S(2)}) collective-permute-start(f32[4,16384]{1,0:T(4,128)S(1)} %pad_maximum_fusion.7), channel_id=1, source_target_pairs={{8,0},{16,8},{24,16},{32,24},{40,32},{48,40},{56,48},{64,56},{72,6... | collective-permute-start | bytes 786440 | tf_op jit(solution)/shard_map/while/body/eval_jaxpr/ppermute | solution.py:13
  204.0 11.5 %collective-permute-start = (f32[4,16384]{1,0:T(4,128)S(1)}, f32[4,16384]{1,0:T(4,128)S(1)}, u32[]{:S(2)}, u32[]{:S(2)}) collective-permute-start(f32[4,16384]{1,0:T(4,128)S(1)} %pad_maximum_fusion.7), channel_id=1, source_target_pairs={{8,0},{16,8},{24,16},{32,24},{40,32},{48,40},{56,48},{64,56},{72,6... | collective-permute-start | bytes 786440 | tf_op jit(solution)/shard_map/while/body/eval_jaxpr/ppermute | solution.py:13
  228.8 10.4 %collective-permute-start = (f32[4,16384]{1,0:T(4,128)S(1)}, f32[4,16384]{1,0:T(4,128)S(1)}, u32[]{:S(2)}, u32[]{:S(2)}) collective-permute-start(f32[4,16384]{1,0:T(4,128)S(1)} %pad_maximum_fusion.7), channel_id=1, source_target_pairs={{8,0},{16,8},{24,16},{32,24},{40,32},{48,40},{56,48},{64,56},{72,6... | collective-permute-start | bytes 786440 | tf_op jit(solution)/shard_map/while/body/eval_jaxpr/ppermute | solution.py:13
  240.6 10.4 %collective-permute-start = (f32[4,16384]{1,0:T(4,128)S(1)}, f32[4,16384]{1,0:T(4,128)S(1)}, u32[]{:S(2)}, u32[]{:S(2)}) collective-permute-start(f32[4,16384]{1,0:T(4,128)S(1)} %pad_maximum_fusion.7), channel_id=1, source_target_pairs={{8,0},{16,8},{24,16},{32,24},{40,32},{48,40},{56,48},{64,56},{72,6... | collective-permute-start | bytes 786440 | tf_op jit(solution)/shard_map/while/body/eval_jaxpr/ppermute | solution.py:13
  264.3 10.4 %collective-permute-start = (f32[4,16384]{1,0:T(4,128)S(1)}, f32[4,16384]{1,0:T(4,128)S(1)}, u32[]{:S(2)}, u32[]{:S(2)}) collective-permute-start(f32[4,16384]{1,0:T(4,128)S(1)} %pad_maximum_fusion.7), channel_id=1, source_target_pairs={{8,0},{16,8},{24,16},{32,24},{40,32},{48,40},{56,48},{64,56},{72,6... | collective-permute-start | bytes 786440 | tf_op jit(solution)/shard_map/while/body/eval_jaxpr/ppermute | solution.py:13
  276.2 10.4 %collective-permute-start = (f32[4,16384]{1,0:T(4,128)S(1)}, f32[4,16384]{1,0:T(4,128)S(1)}, u32[]{:S(2)}, u32[]{:S(2)}) collective-permute-start(f32[4,16384]{1,0:T(4,128)S(1)} %pad_maximum_fusion.7), channel_id=1, source_target_pairs={{8,0},{16,8},{24,16},{32,24},{40,32},{48,40},{56,48},{64,56},{72,6... | collective-permute-start | bytes 786440 | tf_op jit(solution)/shard_map/while/body/eval_jaxpr/ppermute | solution.py:13
  288.1 10.4 %collective-permute-start = (f32[4,16384]{1,0:T(4,128)S(1)}, f32[4,16384]{1,0:T(4,128)S(1)}, u32[]{:S(2)}, u32[]{:S(2)}) collective-permute-start(f32[4,16384]{1,0:T(4,128)S(1)} %pad_maximum_fusion.7), channel_id=1, source_target_pairs={{8,0},{16,8},{24,16},{32,24},{40,32},{48,40},{56,48},{64,56},{72,6... | collective-permute-start | bytes 786440 | tf_op jit(solution)/shard_map/while/body/eval_jaxpr/ppermute | solution.py:13
  299.9 11.2 %collective-permute-start = (f32[4,16384]{1,0:T(4,128)S(1)}, f32[4,16384]{1,0:T(4,128)S(1)}, u32[]{:S(2)}, u32[]{:S(2)}) collective-permute-start(f32[4,16384]{1,0:T(4,128)S(1)} %pad_maximum_fusion.7), channel_id=1, source_target_pairs={{8,0},{16,8},{24,16},{32,24},{40,32},{48,40},{56,48},{64,56},{72,6... | collective-permute-start | bytes 786440 | tf_op jit(solution)/shard_map/while/body/eval_jaxpr/ppermute | solution.py:13
  312.5 12.3 %collective-permute-start = (f32[4,16384]{1,0:T(4,128)S(1)}, f32[4,16384]{1,0:T(4,128)S(1)}, u32[]{:S(2)}, u32[]{:S(2)}) collective-permute-start(f32[4,16384]{1,0:T(4,128)S(1)} %pad_maximum_fusion.7), channel_id=1, source_target_pairs={{8,0},{16,8},{24,16},{32,24},{40,32},{48,40},{56,48},{64,56},{72,6... | collective-permute-start | bytes 786440 | tf_op jit(solution)/shard_map/while/body/eval_jaxpr/ppermute | solution.py:13
  326.3 13.3 %collective-permute-start = (f32[4,16384]{1,0:T(4,128)S(1)}, f32[4,16384]{1,0:T(4,128)S(1)}, u32[]{:S(2)}, u32[]{:S(2)}) collective-permute-start(f32[4,16384]{1,0:T(4,128)S(1)} %pad_maximum_fusion.7), channel_id=1, source_target_pairs={{8,0},{16,8},{24,16},{32,24},{40,32},{48,40},{56,48},{64,56},{72,6... | collective-permute-start | bytes 786440 | tf_op jit(solution)/shard_map/while/body/eval_jaxpr/ppermute | solution.py:13
  341.0 12.4 %collective-permute-start = (f32[4,16384]{1,0:T(4,128)S(1)}, f32[4,16384]{1,0:T(4,128)S(1)}, u32[]{:S(2)}, u32[]{:S(2)}) collective-permute-start(f32[4,16384]{1,0:T(4,128)S(1)} %pad_maximum_fusion.7), channel_id=1, source_target_pairs={{8,0},{16,8},{24,16},{32,24},{40,32},{48,40},{56,48},{64,56},{72,6... | collective-permute-start | bytes 786440 | tf_op jit(solution)/shard_map/while/body/eval_jaxpr/ppermute | solution.py:13
  354.9 11.6 %collective-permute-start = (f32[4,16384]{1,0:T(4,128)S(1)}, f32[4,16384]{1,0:T(4,128)S(1)}, u32[]{:S(2)}, u32[]{:S(2)}) collective-permute-start(f32[4,16384]{1,0:T(4,128)S(1)} %pad_maximum_fusion.7), channel_id=1, source_target_pairs={{8,0},{16,8},{24,16},{32,24},{40,32},{48,40},{56,48},{64,56},{72,6... | collective-permute-start | bytes 786440 | tf_op jit(solution)/shard_map/while/body/eval_jaxpr/ppermute | solution.py:13
  367.9 10.7 %collective-permute-start = (f32[4,16384]{1,0:T(4,128)S(1)}, f32[4,16384]{1,0:T(4,128)S(1)}, u32[]{:S(2)}, u32[]{:S(2)}) collective-permute-start(f32[4,16384]{1,0:T(4,128)S(1)} %pad_maximum_fusion.7), channel_id=1, source_target_pairs={{8,0},{16,8},{24,16},{32,24},{40,32},{48,40},{56,48},{64,56},{72,6... | collective-permute-start | bytes 786440 | tf_op jit(solution)/shard_map/while/body/eval_jaxpr/ppermute | solution.py:13
  380.1 10.4 %collective-permute-start = (f32[4,16384]{1,0:T(4,128)S(1)}, f32[4,16384]{1,0:T(4,128)S(1)}, u32[]{:S(2)}, u32[]{:S(2)}) collective-permute-start(f32[4,16384]{1,0:T(4,128)S(1)} %pad_maximum_fusion.7), channel_id=1, source_target_pairs={{8,0},{16,8},{24,16},{32,24},{40,32},{48,40},{56,48},{64,56},{72,6... | collective-permute-start | bytes 786440 | tf_op jit(solution)/shard_map/while/body/eval_jaxpr/ppermute | solution.py:13
  391.9 10.4 %collective-permute-start = (f32[4,16384]{1,0:T(4,128)S(1)}, f32[4,16384]{1,0:T(4,128)S(1)}, u32[]{:S(2)}, u32[]{:S(2)}) collective-permute-start(f32[4,16384]{1,0:T(4,128)S(1)} %pad_maximum_fusion.7), channel_id=1, source_target_pairs={{8,0},{16,8},{24,16},{32,24},{40,32},{48,40},{56,48},{64,56},{72,6... | collective-permute-start | bytes 786440 | tf_op jit(solution)/shard_map/while/body/eval_jaxpr/ppermute | solution.py:13
  403.8 10.4 %collective-permute-start = (f32[4,16384]{1,0:T(4,128)S(1)}, f32[4,16384]{1,0:T(4,128)S(1)}, u32[]{:S(2)}, u32[]{:S(2)}) collective-permute-start(f32[4,16384]{1,0:T(4,128)S(1)} %pad_maximum_fusion.7), channel_id=1, source_target_pairs={{8,0},{16,8},{24,16},{32,24},{40,32},{48,40},{56,48},{64,56},{72,6... | collective-permute-start | bytes 786440 | tf_op jit(solution)/shard_map/while/body/eval_jaxpr/ppermute | solution.py:13
  415.7 10.4 %collective-permute-start = (f32[4,16384]{1,0:T(4,128)S(1)}, f32[4,16384]{1,0:T(4,128)S(1)}, u32[]{:S(2)}, u32[]{:S(2)}) collective-permute-start(f32[4,16384]{1,0:T(4,128)S(1)} %pad_maximum_fusion.7), channel_id=1, source_target_pairs={{8,0},{16,8},{24,16},{32,24},{40,32},{48,40},{56,48},{64,56},{72,6... | collective-permute-start | bytes 786440 | tf_op jit(solution)/shard_map/while/body/eval_jaxpr/ppermute | solution.py:13
  443.1 43.8 %all-to-all-start.1 = ((f32[8,32,2,128]{3,2,1,0:T(2,128)}), f32[8,32,2,128]{3,2,1,0:T(2,128)S(1)}, u32[]{:S(2)}, u32[]{:S(2)}) async-start(f32[8,32,2,128]{3,2,1,0:T(2,128)} %bitcast.21), calls=%async_computation.1 | async-start | bytes 524288 | tf_op jit(solution)/shard_map/all_to_all | solution.py:111
  (10 other events, 65.0 us)
